TPU v7x, 32 devices: a whole 2x2x4 slice. The times are simulated.
32 devices in a mesh: region: 2 (over x), shard: 16 (over z, y, core).
Axes of the slice: x: 2, y: 2, z: 4, core: 2. Of those that a mesh axis runs over, the one named last changes fastest.
Arguments:
- queries: bfloat16 [48, 1024], replicated, may hold values from -6 to 6
- database: bfloat16 [16384, 1024], P(('region', 'shard')), may hold values from -6 to 6
- neighbour_ids: int32 [48, 10], replicated, may hold values from 0 to 16383
- tile_weights: bfloat16 [64, 13, 4, 256], P(('region', 'shard')), may hold values from 0.0019989014 to 0.059814453
- tile_columns: int32 [64, 13, 4, 256], P(('region', 'shard')), may hold values from 0 to 255
- tile_owner: int32 [64, 13], P(('region', 'shard')), may hold values from 0 to 15, all different within a row; in each aligned block of 2 rows (0 to 1, 2 to 3, ...) at most 2 rows name the same one
- tile_block: int32 [64, 13], P(('region', 'shard')), may hold values from 0 to 1
Outputs:
- diffused: float32 [48, 16384], P(None, ('region', 'shard'))
Inputs may be any that keep to these rules, and one draw needn't show every extreme that they name: `tile_owner`: each row names 13 different owners; among the rows of one device's blocks no owner is named more than 2 times, and that many in some devices.
All inputs are finite; a program needn't handle non-finite values.
Results may differ from a plain program's by a relative error of at most 0.005.
Values may be sent and summed in bfloat16 or wider, within the bound.
A program may use at most 64 MiB of HBM per device.

v0:
```python
import math
import jax
import jax.numpy as jnp
from jax import lax
from jax.sharding import PartitionSpec as P

EPS = 1e-06
BETA = 0.8


def unit_rows(matrix):
    return matrix / jnp.sqrt(jnp.sum(matrix * matrix, axis=1, keepdims=True) + EPS)


def per_device(
    queries, database, neighbour_ids, tile_weights, tile_columns, tile_owner, tile_block
):
    rows_dev = database.shape[0]
    feature_width = database.shape[1]
    unit_query = unit_rows(queries.astype(jnp.float32)).astype(jnp.bfloat16)
    first_row = lax.axis_index(("region", "shard")) * rows_dev
    similar = lax.dot_general(
        unit_query, database, (((1,), (1,)), ((), ())), preferred_element_type=jnp.float32
    )
    positive = jnp.maximum(similar, 0.0)
    weights = (positive * positive * positive / math.sqrt(feature_width)).astype(jnp.bfloat16)
    local_ids = neighbour_ids - first_row
    row_ids = lax.broadcasted_iota(jnp.int32, (1, 1, rows_dev), 2)
    counts = jnp.sum((local_ids[:, :, None] == row_ids).astype(jnp.float32), axis=1)
    chosen = (counts * weights.astype(jnp.float32)).astype(jnp.bfloat16)
    local_term = jnp.dot(chosen, database, preferred_element_type=jnp.float32)
    expanded_sum = lax.psum(local_term, ("region", "shard")) + unit_query.astype(jnp.float32)
    expanded = unit_rows(expanded_sum).astype(jnp.bfloat16)
    products = lax.dot_general(
        expanded, database, (((1,), (1,)), ((), ())), preferred_element_type=jnp.float32
    )
    scores = jnp.maximum(products, 0.0).astype(jnp.bfloat16)
    blocks_dev = tile_columns.shape[0]
    tile_count = tile_columns.shape[1]
    edge_count = tile_columns.shape[2]
    block_rows = tile_columns.shape[3]
    query_count = scores.shape[0]
    score_blocks = scores.reshape(query_count, blocks_dev, block_rows)
    owners = tile_owner.reshape(-1)
    block_ids = tile_block.reshape(-1)
    sources = owners * blocks_dev + block_ids

    def fetch_blocks(current):
        region_blocks = lax.all_gather(current, "shard", axis=1, tiled=True)
        return region_blocks.reshape(query_count, -1)

    column_base = (sources * block_rows).reshape(blocks_dev, tile_count, 1, 1)
    flat_columns = column_base + tile_columns

    def spread(current):
        flat = fetch_blocks(current)
        total = jnp.zeros((query_count, blocks_dev, block_rows), jnp.float32)
        for edge in range(edge_count):
            reached = jnp.take(flat, flat_columns[:, :, edge, :], axis=1)
            scaled = (
                reached.astype(jnp.float32) * tile_weights[:, :, edge, :].astype(jnp.float32)[None]
            )
            total = total + jnp.sum(scaled, axis=2)
        return total

    source = score_blocks.astype(jnp.float32)
    current = score_blocks
    current = (source + BETA * spread(current)).astype(jnp.bfloat16)
    diffused = source + BETA * spread(current)
    return diffused.reshape(query_count, blocks_dev * block_rows)


def solution(mesh):
    placed = (
        P(),
        P(("region", "shard"), None),
        P(),
        P(("region", "shard"), None, None, None),
        P(("region", "shard"), None, None, None),
        P(("region", "shard"), None),
        P(("region", "shard"), None),
    )
    return jax.shard_map(
        per_device,
        mesh=mesh,
        in_specs=placed,
        out_specs=P(None, ("region", "shard")),
        check_vma=False,
    )
```

profile of v0, /device:TPU:0, one launch (start us, length us, event | category | flops | bytes accessed | tf_op | source)
XLA Modules:
  0.0 358.0 jit_solution(2654204438736871811)
XLA Ops:
  6.5 0.0 all-reduce.2.cloned.1.call-start
  6.6 0.8 broadcast_subtract_fusion
  7.4 0.2 convert_reduce_fusion
  7.5 1.0 fusion.1
  8.6 0.0 copy-start.16
  8.6 2.3 fusion.8
  10.9 0.0 all-reduce.2.cloned.1.call-update
  10.9 0.0 copy-done.25
  10.9 0.0 copy-done.24
  11.0 0.1 broadcast_add_fusion
  11.1 0.1 fusion.21
  11.1 0.1 compare_and_fusion
  11.3 0.1 fusion.22
  11.4 0.1 compare_and_fusion.2
  11.5 0.6 pad_clamp_fusion.2
  12.1 0.6 copy.164
  12.7 0.6 pad_clamp_fusion.1
  13.3 0.6 copy.172
  13.9 0.6 copy.179
  14.5 0.6 fusion.14
  15.2 0.6 fusion.12
  15.8 0.6 pad_clamp_fusion
  16.4 123.9 %all-reduce.2.cloned.1.call-done = f32[48,1024]{1,0:T(8,128)} async-done(((f32[48,1024]{1,0:T(8,128)}), f32[48,1024]{1,0:T(8,128)}) %all-reduce.2.cloned.1.call-update) | async-done | bytes 196624 | tf_op jit(solution)/shard_map/psum | solution.py:32
  140.3 1.1 multiply_reduce_fusion.8
  141.4 1.4 fusion
  142.8 25.9 %all_gather.6 = bf16[48,32,256]{2,0,1:T(8,128)(2,1)} all-gather(bf16[48,2,256]{2,0,1:T(8,128)(2,1)S(1)} %bitcast.89), channel_id=1, replica_groups=mesh['region'=2,'shard'=16] {'shard'}, dimensions={1}, use_global_device_ids=true | all-gather | bytes 835584 | tf_op jit(solution)/shard_map/all_gather | solution.py:49
  168.7 2.0 copy.158
  170.7 14.2 %gather_fusion = bf16[6656,48]{1,0:T(8,128)(2,1)} fusion(bf16[48,8192]{0,1:T(8,128)(2,1)S(1)} %bitcast.70, s32[7168]{0:T(1024)S(1)} %pad_clamp_fusion.3), kind=kCustom, calls=%fused_computation.clone | custom fusion | bytes 1304576 | tf_op jit(solution)/shard_map/jit(_take)/gather | solution.py:59
  184.9 0.0 copy-done.14
  184.9 5.3 %multiply_reduce_fusion.7 = f32[48,2,256]{0,2,1:T(8,128)S(1)} fusion(bf16[2,13,256,48]{3,2,1,0:T(8,128)(2,1)} %bitcast.84, f32[2,13,256]{2,1,0:T(8,128)S(1)} %get-tuple-element.29, pred[2,13,256]{2,1,0:T(8,128)(4,1)S(1)} %copy.154), kind=kLoop, calls=%fused_computation.15 | loop fusion | flops 1253376 | bytes 770560 | tf_op jit(solution)/shard_map/reduce_sum | solution.py:63
  190.2 0.1 copy.169
  190.3 15.4 %gather_fusion.1 = bf16[6656,48]{1,0:T(8,128)(2,1)} fusion(bf16[48,8192]{0,1:T(8,128)(2,1)S(1)} %bitcast.71, s32[7168]{0:T(1024)} %pad_clamp_fusion.2), kind=kCustom, calls=%fused_computation.1.clone | custom fusion | bytes 1304576 | tf_op jit(solution)/shard_map/jit(_take)/gather | solution.py:59
  205.7 5.4 %multiply_reduce_fusion.6 = f32[48,2,256]{0,2,1:T(8,128)S(1)} fusion(bf16[2,13,256,48]{3,2,1,0:T(8,128)(2,1)} %bitcast.83, f32[2,13,256]{2,1,0:T(8,128)} %get-tuple-element.28, pred[2,13,256]{2,1,0:T(8,128)(4,1)} %copy.164), kind=kLoop, calls=%fused_computation.14 | loop fusion | flops 1253376 | bytes 770560 | tf_op jit(solution)/shard_map/reduce_sum | solution.py:63
  211.1 0.7 copy.170
  211.8 15.4 %gather_fusion.2 = bf16[6656,48]{1,0:T(8,128)(2,1)} fusion(bf16[48,8192]{0,1:T(8,128)(2,1)S(1)} %bitcast.72, s32[7168]{0:T(1024)} %pad_clamp_fusion.1), kind=kCustom, calls=%fused_computation.2.clone | custom fusion | bytes 1304576 | tf_op jit(solution)/shard_map/jit(_take)/gather | solution.py:59
  227.2 5.4 %multiply_reduce_fusion.5 = f32[48,2,256]{0,2,1:T(8,128)S(1)} fusion(bf16[2,13,256,48]{3,2,1,0:T(8,128)(2,1)} %bitcast.85, f32[2,13,256]{2,1,0:T(8,128)} %get-tuple-element.27, pred[2,13,256]{2,1,0:T(8,128)(4,1)} %copy.172), kind=kLoop, calls=%fused_computation.13 | loop fusion | flops 1253376 | bytes 770560 | tf_op jit(solution)/shard_map/reduce_sum | solution.py:63
  232.6 0.8 copy.177
  233.4 15.5 %gather_fusion.3 = bf16[6656,48]{1,0:T(8,128)(2,1)} fusion(bf16[48,8192]{0,1:T(8,128)(2,1)S(1)} %bitcast.73, s32[7168]{0:T(1024)} %pad_clamp_fusion), kind=kCustom, calls=%fused_computation.3.clone | custom fusion | bytes 1304576 | tf_op jit(solution)/shard_map/jit(_take)/gather | solution.py:59
  248.9 0.0 copy-done.22
  248.9 5.4 %multiply_reduce_fusion.4 = f32[48,2,256]{0,2,1:T(8,128)S(1)} fusion(bf16[2,13,256,48]{3,2,1,0:T(8,128)(2,1)} %bitcast.82, f32[2,13,256]{2,1,0:T(8,128)S(1)} %copy-done.11, pred[2,13,256]{2,1,0:T(8,128)(4,1)S(1)} %copy-done.22), kind=kLoop, calls=%fused_computation.12 | loop fusion | flops 1253376 | bytes 770560 | tf_op jit(solution)/shard_map/reduce_sum | solution.py:63
  254.3 0.1 copy.184
  254.4 0.0 copy-done.4
  254.5 21.0 %all_gather.7 = bf16[48,32,256]{2,0,1:T(8,128)(2,1)} all-gather(bf16[48,2,256]{2,0,1:T(8,128)(2,1)S(1)} %add_convert_fusion), channel_id=1, replica_groups=mesh['region'=2,'shard'=16] {'shard'}, dimensions={1}, use_global_device_ids=true | all-gather | bytes 835584 | tf_op jit(solution)/shard_map/all_gather | solution.py:49
  275.5 2.0 copy.185
  277.4 0.0 copy-done.7
  277.5 0.0 copy-start.8
  277.5 14.2 %gather_fusion.4 = bf16[6656,48]{1,0:T(8,128)(2,1)} fusion(bf16[48,8192]{0,1:T(8,128)(2,1)S(1)} %bitcast.74, s32[7168]{0:T(1024)S(1)} %copy-done.7), kind=kCustom, calls=%fused_computation.4.clone | custom fusion | bytes 1304576 | tf_op jit(solution)/shard_map/jit(_take)/gather | solution.py:59
  291.6 0.0 copy-done.8
  291.6 14.1 %gather_fusion.5 = bf16[6656,48]{1,0:T(8,128)(2,1)} fusion(bf16[48,8192]{0,1:T(8,128)(2,1)S(1)} %bitcast.75, s32[7168]{0:T(1024)S(1)} %copy-done.8), kind=kCustom, calls=%fused_computation.5.clone | custom fusion | bytes 1304576 | tf_op jit(solution)/shard_map/jit(_take)/gather | solution.py:59
  305.8 14.1 %gather_fusion.6 = bf16[6656,48]{1,0:T(8,128)(2,1)} fusion(bf16[48,8192]{0,1:T(8,128)(2,1)S(1)} %bitcast.76, s32[7168]{0:T(1024)S(1)} %copy-done.9), kind=kCustom, calls=%fused_computation.6.clone | custom fusion | bytes 1304576 | tf_op jit(solution)/shard_map/jit(_take)/gather | solution.py:59
  319.9 0.0 copy-done.10
  319.9 14.2 %gather_fusion.7 = bf16[6656,48]{1,0:T(8,128)(2,1)} fusion(bf16[48,8192]{0,1:T(8,128)(2,1)S(1)} %bitcast.77, s32[7168]{0:T(1024)S(1)} %copy-done.10), kind=kCustom, calls=%fused_computation.7.clone | custom fusion | bytes 1304576 | tf_op jit(solution)/shard_map/jit(_take)/gather | solution.py:59
  334.1 5.5 %multiply_reduce_fusion.3 = f32[48,2,256]{0,2,1:T(8,128)S(1)} fusion(bf16[2,13,256,48]{3,2,1,0:T(8,128)(2,1)} %bitcast.81, f32[2,13,256]{2,1,0:T(8,128)S(1)} %copy-done.15, pred[2,13,256]{2,1,0:T(8,128)(4,1)S(1)} %copy-done.19), kind=kLoop, calls=%fused_computation.11 | loop fusion | flops 1253376 | bytes 770560 | tf_op jit(solution)/shard_map/reduce_sum | solution.py:63
  339.6 0.1 copy.189
  339.7 0.0 copy-done.2
  339.7 2.4 multiply_reduce_fusion.2
  342.2 0.1 copy.190
  342.3 0.0 copy-done.12
  342.3 5.4 %multiply_reduce_fusion.1 = f32[48,2,256]{0,2,1:T(8,128)S(1)} fusion(bf16[2,13,256,48]{3,2,1,0:T(8,128)(2,1)} %bitcast.79, f32[2,13,256]{2,1,0:T(8,128)S(1)} %copy-done.12, pred[2,13,256]{2,1,0:T(8,128)(4,1)S(1)} %copy-done.21), kind=kLoop, calls=%fused_computation.9 | loop fusion | flops 1253376 | bytes 770560 | tf_op jit(solution)/shard_map/reduce_sum | solution.py:63
  347.7 0.1 copy.193
  347.9 0.0 copy-done.1
  347.9 2.4 multiply_reduce_fusion
  350.3 0.1 copy.196
  350.5 0.7 convert_add_fusion.1
  (56 shorter events, 0.2 us)
Async XLA Ops:
  6.5 2.0 copy-start
  6.5 4.4 %copy-start.25 = (s32[2,13]{1,0:T(2,128)S(1)}, s32[2,13]{1,0:T(2,128)}, u32[]{:S(2)}) copy-start(s32[2,13]{1,0:T(2,128)} %param.14) | copy-start | bytes 316
  6.5 4.4 %copy-start.24 = (s32[2,13]{1,0:T(2,128)S(1)}, s32[2,13]{1,0:T(2,128)}, u32[]{:S(2)}) copy-start(s32[2,13]{1,0:T(2,128)} %param.15) | copy-start | bytes 316
  6.5 4.4 %copy-start.17 = (s32[2,13,4,256]{3,2,1,0:T(4,128)S(1)}, s32[2,13,4,256]{3,2,1,0:T(4,128)}, u32[]{:S(2)}) copy-start(s32[2,13,4,256]{3,2,1,0:T(4,128)} %param.13) | copy-start | bytes 319492
  6.5 133.7 %all-reduce.2.cloned.1.call-start = ((), (), s32[]{:S(2)}) async-start(), calls=%async_computation | async-start | bytes 393216 | tf_op jit(solution)/shard_map/psum | solution.py:32
  8.6 2.7 copy-start.16
  10.9 129.4 %copy-start.3 = (bf16[48,1024]{1,0:T(8,128)(2,1)S(1)}, bf16[48,1024]{1,0:T(8,128)(2,1)}, u32[]{:S(2)}) copy-start(bf16[48,1024]{1,0:T(8,128)(2,1)} %param.9) | copy-start | bytes 294916
  11.3 159.5 %copy-start.6 = (s32[7168]{0:T(1024)}, s32[7168]{0:T(1024)S(1)}, u32[]{:S(2)}) copy-start(s32[7168]{0:T(1024)S(1)} %pad_clamp_fusion.3) | copy-start | bytes 86020
  11.3 173.6 %copy-start.18 = (pred[2,13,256]{2,1,0:T(8,128)(4,1)}, pred[2,13,256]{2,1,0:T(8,128)(4,1)S(1)}, u32[]{:S(2)}) copy-start(pred[2,13,256]{2,1,0:T(8,128)(4,1)S(1)} %copy.154) | copy-start | bytes 19972
  15.2 169.7 %copy-start.14 = (f32[2,13,256]{2,1,0:T(8,128)}, f32[2,13,256]{2,1,0:T(8,128)S(1)}, u32[]{:S(2)}) copy-start(f32[2,13,256]{2,1,0:T(8,128)S(1)} %get-tuple-element.29) | copy-start | bytes 79876
  233.4 15.5 %copy-start.11 = (f32[2,13,256]{2,1,0:T(8,128)S(1)}, f32[2,13,256]{2,1,0:T(8,128)}, u32[]{:S(2)}) copy-start(f32[2,13,256]{2,1,0:T(8,128)} %get-tuple-element.26) | copy-start | bytes 79876
  233.4 15.5 %copy-start.22 = (pred[2,13,256]{2,1,0:T(8,128)(4,1)S(1)}, pred[2,13,256]{2,1,0:T(8,128)(4,1)}, u32[]{:S(2)}) copy-start(pred[2,13,256]{2,1,0:T(8,128)(4,1)} %copy.179) | copy-start | bytes 19972
  248.9 5.5 %copy-start.4 = (f32[48,2,256]{2,0,1:T(8,128)S(1)}, f32[48,2,256]{2,0,1:T(8,128)}, u32[]{:S(2)}) copy-start(f32[48,2,256]{2,0,1:T(8,128)} %copy.170) | copy-start | bytes 294916
  248.9 5.5 %copy-start.5 = (f32[48,2,256]{2,0,1:T(8,128)S(1)}, f32[48,2,256]{2,0,1:T(8,128)}, u32[]{:S(2)}) copy-start(f32[48,2,256]{2,0,1:T(8,128)} %copy.177) | copy-start | bytes 294916
  254.4 23.0 %copy-start.7 = (s32[7168]{0:T(1024)S(1)}, s32[7168]{0:T(1024)}, u32[]{:S(2)}) copy-start(s32[7168]{0:T(1024)} %copy-done.6) | copy-start | bytes 86020
  277.5 14.2 %copy-start.8 = (s32[7168]{0:T(1024)S(1)}, s32[7168]{0:T(1024)}, u32[]{:S(2)}) copy-start(s32[7168]{0:T(1024)} %pad_clamp_fusion.2) | copy-start | bytes 86020
  291.6 14.1 %copy-start.9 = (s32[7168]{0:T(1024)S(1)}, s32[7168]{0:T(1024)}, u32[]{:S(2)}) copy-start(s32[7168]{0:T(1024)} %pad_clamp_fusion.1) | copy-start | bytes 86020
  305.8 14.2 %copy-start.10 = (s32[7168]{0:T(1024)S(1)}, s32[7168]{0:T(1024)}, u32[]{:S(2)}) copy-start(s32[7168]{0:T(1024)} %pad_clamp_fusion) | copy-start | bytes 86020
  319.9 14.2 %copy-start.15 = (f32[2,13,256]{2,1,0:T(8,128)S(1)}, f32[2,13,256]{2,1,0:T(8,128)}, u32[]{:S(2)}) copy-start(f32[2,13,256]{2,1,0:T(8,128)} %copy-done.14) | copy-start | bytes 79876
  319.9 14.2 %copy-start.19 = (pred[2,13,256]{2,1,0:T(8,128)(4,1)S(1)}, pred[2,13,256]{2,1,0:T(8,128)(4,1)}, u32[]{:S(2)}) copy-start(pred[2,13,256]{2,1,0:T(8,128)(4,1)} %copy-done.18) | copy-start | bytes 19972
  334.1 5.6 %copy-start.2 = (bf16[6656,48]{1,0:T(8,128)(2,1)S(1)}, bf16[6656,48]{1,0:T(8,128)(2,1)}, u32[]{:S(2)}) copy-start(bf16[6656,48]{1,0:T(8,128)(2,1)} %gather_fusion.5) | copy-start | bytes 1916932
  334.1 5.6 %copy-start.13 = (f32[2,13,256]{2,1,0:T(8,128)S(1)}, f32[2,13,256]{2,1,0:T(8,128)}, u32[]{:S(2)}) copy-start(f32[2,13,256]{2,1,0:T(8,128)} %get-tuple-element.28) | copy-start | bytes 79876
  334.1 5.6 %copy-start.20 = (pred[2,13,256]{2,1,0:T(8,128)(4,1)S(1)}, pred[2,13,256]{2,1,0:T(8,128)(4,1)}, u32[]{:S(2)}) copy-start(pred[2,13,256]{2,1,0:T(8,128)(4,1)} %copy.164) | copy-start | bytes 19972
  339.6 2.7 copy-start.12
  339.6 2.7 copy-start.21
  342.1 5.7 %copy-start.1 = (bf16[6656,48]{1,0:T(8,128)(2,1)S(1)}, bf16[6656,48]{1,0:T(8,128)(2,1)}, u32[]{:S(2)}) copy-start(bf16[6656,48]{1,0:T(8,128)(2,1)} %gather_fusion.7) | copy-start | bytes 1916932
  342.2 5.7 %copy-start.23 = (pred[2,13,256]{2,1,0:T(8,128)(4,1)S(1)}, pred[2,13,256]{2,1,0:T(8,128)(4,1)}, u32[]{:S(2)}) copy-start(pred[2,13,256]{2,1,0:T(8,128)(4,1)} %copy.179) | copy-start | bytes 19972
Sparse Core Ops, SparseCore 0:
  12.9 127.3 all-reduce.1
where the time goes:
time: 360 us; the launch traced here: 358 us
  local copies, waits for them, and re-layouts  125 us (35%)
  waiting for transfers between devices  124 us (34%)
  blocking collectives  46.9 us (13%)
  other arithmetic  44.3 us (12%)
  between operations  13.9 us (4%)
  matrix products  3.67 us (1%)
    psum x1, waiting for transfers between devices, per_device(): lax.psum(local_term, ('region', 'shard')) + unit_query.astype(jnp.float32)  124 us
    gather x8, local copies, waits for them, and re-layouts, spread(): reached = jnp.take(flat, flat_columns[:, :, edge, :], axis=1)  117 us
    all_gather x2, blocking collectives, fetch_blocks(): region_blocks = lax.all_gather(current, 'shard', axis=1, tiled=True)  46.9 us
    reduce_sum x8, other arithmetic, spread(): total = total + jnp.sum(scaled, axis=2)  37.2 us
  transfers between devices with their start and end apart: 1, of which 1 were waited for; matrix products, arithmetic and copies ran while one was open for 1% of the time, Pallas kernels for 0%

commit v1 on v0

--- a/solution.py
+++ b/solution.py
@@ -46,7 +46,25 @@
     sources = owners * blocks_dev + block_ids
 
     def fetch_blocks(current):
-        region_blocks = lax.all_gather(current, "shard", axis=1, tiled=True)
+        ways, here, hop = (lax.axis_size("shard"), lax.axis_index("shard"), current.shape[1])
+        lengths = [n * ways if d == 1 else n for d, n in enumerate(current.shape)]
+        full = lax.dynamic_update_slice_in_dim(
+            jnp.zeros(lengths, current.dtype), current, here * hop, axis=1
+        )
+        going_up = going_down = current
+        for far in range(1, ways // 2 + 1):
+            going_up = lax.ppermute(going_up, "shard", [(d, (d + 1) % ways) for d in range(ways)])
+            full = lax.dynamic_update_slice_in_dim(
+                full, going_up, (here - far) % ways * hop, axis=1
+            )
+            if 2 * far < ways:
+                going_down = lax.ppermute(
+                    going_down, "shard", [(d, (d - 1) % ways) for d in range(ways)]
+                )
+                full = lax.dynamic_update_slice_in_dim(
+                    full, going_down, (here + far) % ways * hop, axis=1
+                )
+        region_blocks = full
         return region_blocks.reshape(query_count, -1)
 
     column_base = (sources * block_rows).reshape(blocks_dev, tile_count, 1, 1)

time: 360 us -> 417 us (1.16)
  starting transfers between devices: 0.03 us -> 63.2 us
  blocking collectives: 46.9 us -> 0 us
  waiting for transfers between devices: 124 us -> 164 us
  local copies, waits for them, and re-layouts: 125 us -> 133 us
  other arithmetic: 44.3 us -> 37 us
    ppermute x0 -> x30, starting transfers between devices: none -> 63.2 us  [the longest x14 62.7 us: fetch_blocks(): lax.ppermute(going_down, 'shard', [(d, (d - 1) % ways) for d in range(way...]
    all_gather x2 -> x0, blocking collectives: 46.9 us -> none  [fetch_blocks(): region_blocks = lax.all_gather(current, 'shard', axis=1, tiled=True)]
    ppermute x0 -> x30, waiting for transfers between devices: none -> 39 us  [the longest x16 39 us: fetch_blocks(): lax.ppermute(going_up, 'shard', [(d, (d + 1) % ways) for d in range(ways)])]
    ppermute x0 -> x15, local copies, waits for them, and re-layouts: none -> 13.9 us  [the longest x8 7.41 us: fetch_blocks(): lax.ppermute(going_up, 'shard', [(d, (d + 1) % ways) for d in range(ways)])]
    reduce_sum x8, other arithmetic: 37.2 us -> 31.5 us  [spread(): total = total + jnp.sum(scaled, axis=2)]
  transfers between devices with their start and end apart: 1 -> 31, of which waited for: 1 -> 17; matrix products, arithmetic and copies ran while one was open for 1% -> 4% of each run, Pallas kernels for 0% -> 0%
where the time goes in v1:
time: 417 us; the launch traced here: 415 us
  waiting for transfers between devices  164 us (39%)
  local copies, waits for them, and re-layouts  133 us (32%)
  starting transfers between devices  63.2 us (15%)
  other arithmetic  37 us (9%)
  between operations  14.5 us (3%)
    psum x1, waiting for transfers between devices, per_device(): lax.psum(local_term, ('region', 'shard')) + unit_query.astype(jnp.float32)  125 us
    gather x8, local copies, waits for them, and re-layouts, spread(): reached = jnp.take(flat, flat_columns[:, :, edge, :], axis=1)  113 us
    ppermute x14, starting transfers between devices, fetch_blocks(): lax.ppermute(going_down, 'shard', [(d, (d - 1) % ways) for d in range(way...  62.7 us
    ppermute x16, waiting for transfers between devices, fetch_blocks(): lax.ppermute(going_up, 'shard', [(d, (d + 1) % ways) for d in range(ways)])  39 us
    reduce_sum x8, other arithmetic, spread(): total = total + jnp.sum(scaled, axis=2)  31.5 us
  transfers between devices with their start and end apart: 31, of which 17 were waited for; matrix products, arithmetic and copies ran while one was open for 4% of the time, Pallas kernels for 0%

profile of v1, /device:TPU:0, one launch (start us, length us, event | category | flops | bytes accessed | tf_op | source)
XLA Modules:
  0.0 415.3 jit_solution(2922876308512405050)
XLA Ops:
  7.6 1.0 fusion.1
  8.6 2.3 fusion.8
  15.5 124.8 %all-reduce.2.cloned.1.call-done = f32[48,1024]{1,0:T(8,128)} async-done(((f32[48,1024]{1,0:T(8,128)}), f32[48,1024]{1,0:T(8,128)}) %all-reduce.2.cloned.1.call-update) | async-done | bytes 196624 | tf_op jit(solution)/shard_map/psum | solution.py:32
  140.3 1.1 multiply_reduce_fusion.8
  141.5 1.4 fusion
  144.5 4.4 %collective-permute-start.1 = (bf16[48,2,256]{2,1,0:T(2,128)(2,1)}, bf16[48,2,256]{2,1,0:T(2,128)(2,1)}, u32[]{:S(2)}, u32[]{:S(2)}) collective-permute-start(bf16[48,2,256]{2,1,0:T(2,128)(2,1)} %reshape.74), channel_id=1, source_target_pairs={{0,15},{1,0},{2,1},{3,2},{4,3},{5,4},{6,5},{7,6},{8,7},{9,8},{10,9... | collective-permute-start | bytes 147464 | tf_op jit(solution)/shard_map/ppermute | solution.py:61
  149.4 1.6 collective-permute-done
  151.0 0.9 copy.200
  152.1 0.9 copy.201
  153.0 4.5 %collective-permute-start.3 = (bf16[48,2,256]{2,1,0:T(2,128)(2,1)}, bf16[48,2,256]{2,1,0:T(2,128)(2,1)}, u32[]{:S(2)}, u32[]{:S(2)}) collective-permute-start(bf16[48,2,256]{2,1,0:T(2,128)(2,1)} %collective-permute-done.1), channel_id=1, source_target_pairs={{0,15},{1,0},{2,1},{3,2},{4,3},{5,4},{6,5},{7,6},{8,7},{9,8},{10,9... | collective-permute-start | bytes 147464 | tf_op jit(solution)/shard_map/ppermute | solution.py:61
  157.5 1.1 collective-permute-done.2
  158.6 0.9 copy.202
  159.6 0.9 copy.203
  160.6 4.5 %collective-permute-start.5 = (bf16[48,2,256]{2,1,0:T(2,128)(2,1)}, bf16[48,2,256]{2,1,0:T(2,128)(2,1)}, u32[]{:S(2)}, u32[]{:S(2)}) collective-permute-start(bf16[48,2,256]{2,1,0:T(2,128)(2,1)} %collective-permute-done.3), channel_id=1, source_target_pairs={{0,15},{1,0},{2,1},{3,2},{4,3},{5,4},{6,5},{7,6},{8,7},{9,8},{10,9... | collective-permute-start | bytes 147464 | tf_op jit(solution)/shard_map/ppermute | solution.py:61
  165.0 1.1 collective-permute-done.4
  166.1 0.9 copy.204
  167.1 0.9 copy.205
  168.1 4.5 %collective-permute-start.7 = (bf16[48,2,256]{2,1,0:T(2,128)(2,1)}, bf16[48,2,256]{2,1,0:T(2,128)(2,1)}, u32[]{:S(2)}, u32[]{:S(2)}) collective-permute-start(bf16[48,2,256]{2,1,0:T(2,128)(2,1)} %collective-permute-done.5), channel_id=1, source_target_pairs={{0,15},{1,0},{2,1},{3,2},{4,3},{5,4},{6,5},{7,6},{8,7},{9,8},{10,9... | collective-permute-start | bytes 147464 | tf_op jit(solution)/shard_map/ppermute | solution.py:61
  172.6 1.1 collective-permute-done.6
  173.6 0.9 copy.206
  174.7 0.9 copy.207
  175.6 4.5 %collective-permute-start.9 = (bf16[48,2,256]{2,1,0:T(2,128)(2,1)}, bf16[48,2,256]{2,1,0:T(2,128)(2,1)}, u32[]{:S(2)}, u32[]{:S(2)}) collective-permute-start(bf16[48,2,256]{2,1,0:T(2,128)(2,1)} %collective-permute-done.7), channel_id=1, source_target_pairs={{0,15},{1,0},{2,1},{3,2},{4,3},{5,4},{6,5},{7,6},{8,7},{9,8},{10,9... | collective-permute-start | bytes 147464 | tf_op jit(solution)/shard_map/ppermute | solution.py:61
  180.1 1.1 collective-permute-done.8
  181.2 0.9 copy.208
  182.2 0.9 copy.209
  183.2 4.5 %collective-permute-start.11 = (bf16[48,2,256]{2,1,0:T(2,128)(2,1)}, bf16[48,2,256]{2,1,0:T(2,128)(2,1)}, u32[]{:S(2)}, u32[]{:S(2)}) collective-permute-start(bf16[48,2,256]{2,1,0:T(2,128)(2,1)} %collective-permute-done.9), channel_id=1, source_target_pairs={{0,15},{1,0},{2,1},{3,2},{4,3},{5,4},{6,5},{7,6},{8,7},{9,8},{10,9... | collective-permute-start | bytes 147464 | tf_op jit(solution)/shard_map/ppermute | solution.py:61
  187.7 1.1 collective-permute-done.10
  189.8 0.9 copy.211
  190.7 4.5 %collective-permute-start.13 = (bf16[48,2,256]{2,1,0:T(2,128)(2,1)}, bf16[48,2,256]{2,1,0:T(2,128)(2,1)}, u32[]{:S(2)}, u32[]{:S(2)}) collective-permute-start(bf16[48,2,256]{2,1,0:T(2,128)(2,1)} %collective-permute-done.11), channel_id=1, source_target_pairs={{0,15},{1,0},{2,1},{3,2},{4,3},{5,4},{6,5},{7,6},{8,7},{9,8},{10,9... | collective-permute-start | bytes 147464 | tf_op jit(solution)/shard_map/ppermute | solution.py:61
  195.2 1.1 collective-permute-done.12
  196.3 0.9 copy.212
  197.3 0.9 copy.213
  198.3 5.5 %collective-permute-done.14 = bf16[48,2,256]{2,1,0:T(2,128)(2,1)} collective-permute-done((bf16[48,2,256]{2,1,0:T(2,128)(2,1)}, bf16[48,2,256]{2,1,0:T(2,128)(2,1)}, u32[]{:S(2)}, u32[]{:S(2)}) %collective-permute-start.14) | collective-permute-done | bytes 49184 | tf_op jit(solution)/shard_map/ppermute | solution.py:56
  204.8 14.1 %gather_fusion.2 = bf16[6656,48]{1,0:T(8,128)(2,1)} fusion(bf16[48,8192]{0,1:T(8,128)(2,1)S(1)} %bitcast.66, s32[7168]{0:T(1024)S(1)} %pad_clamp_fusion.1), kind=kCustom, calls=%fused_computation.2.clone | custom fusion | bytes 1304576 | tf_op jit(solution)/shard_map/jit(_take)/gather | solution.py:77
  218.9 14.2 %gather_fusion.1 = bf16[6656,48]{1,0:T(8,128)(2,1)} fusion(bf16[48,8192]{0,1:T(8,128)(2,1)S(1)} %bitcast.67, s32[7168]{0:T(1024)S(1)} %pad_clamp_fusion.2), kind=kCustom, calls=%fused_computation.1.clone | custom fusion | bytes 1304576 | tf_op jit(solution)/shard_map/jit(_take)/gather | solution.py:77
  233.1 14.1 %gather_fusion = bf16[6656,48]{1,0:T(8,128)(2,1)} fusion(bf16[48,8192]{0,1:T(8,128)(2,1)S(1)} %bitcast.68, s32[7168]{0:T(1024)S(1)} %pad_clamp_fusion.3), kind=kCustom, calls=%fused_computation.clone | custom fusion | bytes 1304576 | tf_op jit(solution)/shard_map/jit(_take)/gather | solution.py:77
  247.2 14.2 %gather_fusion.3 = bf16[6656,48]{1,0:T(8,128)(2,1)} fusion(bf16[48,8192]{0,1:T(8,128)(2,1)S(1)} %bitcast.69, s32[7168]{0:T(1024)S(1)} %pad_clamp_fusion), kind=kCustom, calls=%fused_computation.3.clone | custom fusion | bytes 1304576 | tf_op jit(solution)/shard_map/jit(_take)/gather | solution.py:77
  261.4 5.5 %multiply_reduce_fusion.5 = f32[48,2,256]{0,2,1:T(8,128)S(1)} fusion(bf16[2,13,256,48]{3,2,1,0:T(8,128)(2,1)} %bitcast.77, f32[2,13,256]{2,1,0:T(8,128)S(1)} %copy-done.7, pred[2,13,256]{2,1,0:T(8,128)(4,1)S(1)} %copy-done.13), kind=kLoop, calls=%fused_computation.13 | loop fusion | flops 1253376 | bytes 770560 | tf_op jit(solution)/shard_map/reduce_sum | solution.py:81
  266.9 5.5 %multiply_reduce_fusion.6 = f32[48,2,256]{0,2,1:T(8,128)S(1)} fusion(bf16[2,13,256,48]{3,2,1,0:T(8,128)(2,1)} %bitcast.76, f32[2,13,256]{2,1,0:T(8,128)S(1)} %copy-done.8, pred[2,13,256]{2,1,0:T(8,128)(4,1)S(1)} %copy-done.14), kind=kLoop, calls=%fused_computation.14 | loop fusion | flops 1253376 | bytes 770560 | tf_op jit(solution)/shard_map/reduce_sum | solution.py:81
  272.4 2.4 multiply_reduce_fusion.7
  274.9 2.4 multiply_reduce_fusion.4
  277.9 4.4 %collective-permute-start.16 = (bf16[48,2,256]{0,2,1:T(8,128)(2,1)S(1)}, bf16[48,2,256]{0,2,1:T(8,128)(2,1)S(1)}, u32[]{:S(2)}, u32[]{:S(2)}) collective-permute-start(bf16[48,2,256]{0,2,1:T(8,128)(2,1)S(1)} %get-tuple-element.7), channel_id=1, source_target_pairs={{0,15},{1,0},{2,1},{3,2},{4,3},{5,4},{6,5},{7,6},{8,7},{9,8},{10,9... | collective-permute-start | bytes 147464 | tf_op jit(solution)/shard_map/ppermute | solution.py:61
  282.3 2.7 collective-permute-done.15
  285.1 4.5 %collective-permute-start.18 = (bf16[48,2,256]{0,2,1:T(8,128)(2,1)S(1)}, bf16[48,2,256]{0,2,1:T(8,128)(2,1)S(1)}, u32[]{:S(2)}, u32[]{:S(2)}) collective-permute-start(bf16[48,2,256]{0,2,1:T(8,128)(2,1)S(1)} %collective-permute-done.16), channel_id=1, source_target_pairs={{0,15},{1,0},{2,1},{3,2},{4,3},{5,4},{6,5},{7,6},{8,7},{9,8},{10,9... | collective-permute-start | bytes 147464 | tf_op jit(solution)/shard_map/ppermute | solution.py:61
  289.6 2.6 collective-permute-done.17
  292.3 4.5 %collective-permute-start.20 = (bf16[48,2,256]{0,2,1:T(8,128)(2,1)S(1)}, bf16[48,2,256]{0,2,1:T(8,128)(2,1)S(1)}, u32[]{:S(2)}, u32[]{:S(2)}) collective-permute-start(bf16[48,2,256]{0,2,1:T(8,128)(2,1)S(1)} %collective-permute-done.18), channel_id=1, source_target_pairs={{0,15},{1,0},{2,1},{3,2},{4,3},{5,4},{6,5},{7,6},{8,7},{9,8},{10,9... | collective-permute-start | bytes 147464 | tf_op jit(solution)/shard_map/ppermute | solution.py:61
  296.8 2.6 collective-permute-done.19
  299.5 4.5 %collective-permute-start.22 = (bf16[48,2,256]{0,2,1:T(8,128)(2,1)S(1)}, bf16[48,2,256]{0,2,1:T(8,128)(2,1)S(1)}, u32[]{:S(2)}, u32[]{:S(2)}) collective-permute-start(bf16[48,2,256]{0,2,1:T(8,128)(2,1)S(1)} %collective-permute-done.20), channel_id=1, source_target_pairs={{0,15},{1,0},{2,1},{3,2},{4,3},{5,4},{6,5},{7,6},{8,7},{9,8},{10,9... | collective-permute-start | bytes 147464 | tf_op jit(solution)/shard_map/ppermute | solution.py:61
  304.0 2.6 collective-permute-done.21
  306.7 4.5 %collective-permute-start.24 = (bf16[48,2,256]{0,2,1:T(8,128)(2,1)S(1)}, bf16[48,2,256]{0,2,1:T(8,128)(2,1)S(1)}, u32[]{:S(2)}, u32[]{:S(2)}) collective-permute-start(bf16[48,2,256]{0,2,1:T(8,128)(2,1)S(1)} %collective-permute-done.22), channel_id=1, source_target_pairs={{0,15},{1,0},{2,1},{3,2},{4,3},{5,4},{6,5},{7,6},{8,7},{9,8},{10,9... | collective-permute-start | bytes 147464 | tf_op jit(solution)/shard_map/ppermute | solution.py:61
  311.2 2.6 collective-permute-done.23
  313.9 4.5 %collective-permute-start.26 = (bf16[48,2,256]{0,2,1:T(8,128)(2,1)S(1)}, bf16[48,2,256]{0,2,1:T(8,128)(2,1)S(1)}, u32[]{:S(2)}, u32[]{:S(2)}) collective-permute-start(bf16[48,2,256]{0,2,1:T(8,128)(2,1)S(1)} %collective-permute-done.24), channel_id=1, source_target_pairs={{0,15},{1,0},{2,1},{3,2},{4,3},{5,4},{6,5},{7,6},{8,7},{9,8},{10,9... | collective-permute-start | bytes 147464 | tf_op jit(solution)/shard_map/ppermute | solution.py:61
  318.4 2.6 collective-permute-done.25
  321.1 4.5 %collective-permute-start.28 = (bf16[48,2,256]{0,2,1:T(8,128)(2,1)S(1)}, bf16[48,2,256]{0,2,1:T(8,128)(2,1)S(1)}, u32[]{:S(2)}, u32[]{:S(2)}) collective-permute-start(bf16[48,2,256]{0,2,1:T(8,128)(2,1)S(1)} %collective-permute-done.26), channel_id=1, source_target_pairs={{0,15},{1,0},{2,1},{3,2},{4,3},{5,4},{6,5},{7,6},{8,7},{9,8},{10,9... | collective-permute-start | bytes 147464 | tf_op jit(solution)/shard_map/ppermute | solution.py:61
  325.6 2.5 collective-permute-done.27
  328.2 7.0 %collective-permute-done.29 = bf16[48,2,256]{0,2,1:T(8,128)(2,1)S(1)} collective-permute-done((bf16[48,2,256]{0,2,1:T(8,128)(2,1)S(1)}, bf16[48,2,256]{0,2,1:T(8,128)(2,1)S(1)}, u32[]{:S(2)}, u32[]{:S(2)}) %collective-permute-start.29) | collective-permute-done | bytes 49184 | tf_op jit(solution)/shard_map/ppermute | solution.py:56
  335.2 14.1 %gather_fusion.6 = bf16[6656,48]{1,0:T(8,128)(2,1)} fusion(bf16[48,8192]{0,1:T(8,128)(2,1)S(1)} %bitcast.62, s32[7168]{0:T(1024)S(1)} %pad_clamp_fusion.1), kind=kCustom, calls=%fused_computation.6.clone | custom fusion | bytes 1304576 | tf_op jit(solution)/shard_map/jit(_take)/gather | solution.py:77
  349.4 14.1 %gather_fusion.5 = bf16[6656,48]{1,0:T(8,128)(2,1)} fusion(bf16[48,8192]{0,1:T(8,128)(2,1)S(1)} %bitcast.63, s32[7168]{0:T(1024)S(1)} %pad_clamp_fusion.2), kind=kCustom, calls=%fused_computation.5.clone | custom fusion | bytes 1304576 | tf_op jit(solution)/shard_map/jit(_take)/gather | solution.py:77
  363.5 14.2 %gather_fusion.4 = bf16[6656,48]{1,0:T(8,128)(2,1)} fusion(bf16[48,8192]{0,1:T(8,128)(2,1)S(1)} %bitcast.64, s32[7168]{0:T(1024)S(1)} %pad_clamp_fusion.3), kind=kCustom, calls=%fused_computation.4.clone | custom fusion | bytes 1304576 | tf_op jit(solution)/shard_map/jit(_take)/gather | solution.py:77
  377.7 14.1 %gather_fusion.7 = bf16[6656,48]{1,0:T(8,128)(2,1)} fusion(bf16[48,8192]{0,1:T(8,128)(2,1)S(1)} %bitcast.65, s32[7168]{0:T(1024)S(1)} %pad_clamp_fusion), kind=kCustom, calls=%fused_computation.7.clone | custom fusion | bytes 1304576 | tf_op jit(solution)/shard_map/jit(_take)/gather | solution.py:77
  391.8 5.5 %multiply_reduce_fusion.1 = f32[48,2,256]{0,2,1:T(8,128)S(1)} fusion(bf16[2,13,256,48]{3,2,1,0:T(8,128)(2,1)} %bitcast.73, f32[2,13,256]{2,1,0:T(8,128)S(1)} %copy-done.7, pred[2,13,256]{2,1,0:T(8,128)(4,1)S(1)} %copy-done.13), kind=kLoop, calls=%fused_computation.9 | loop fusion | flops 1253376 | bytes 770560 | tf_op jit(solution)/shard_map/reduce_sum | solution.py:81
  397.3 5.5 %multiply_reduce_fusion.2 = f32[48,2,256]{0,2,1:T(8,128)S(1)} fusion(bf16[2,13,256,48]{3,2,1,0:T(8,128)(2,1)} %bitcast.72, f32[2,13,256]{2,1,0:T(8,128)S(1)} %copy-done.8, pred[2,13,256]{2,1,0:T(8,128)(4,1)S(1)} %copy-done.14), kind=kLoop, calls=%fused_computation.10 | loop fusion | flops 1253376 | bytes 770560 | tf_op jit(solution)/shard_map/reduce_sum | solution.py:81
  402.8 2.4 multiply_reduce_fusion.3
  405.2 2.4 multiply_reduce_fusion
  (139 shorter events, 11.8 us)
Async XLA Ops:
  6.5 2.1 copy-start
  6.5 4.7 %copy-start.18 = (s32[2,13]{1,0:T(2,128)S(1)}, s32[2,13]{1,0:T(2,128)}, u32[]{:S(2)}) copy-start(s32[2,13]{1,0:T(2,128)} %param.14) | copy-start | bytes 316
  6.5 4.7 %copy-start.17 = (s32[2,13]{1,0:T(2,128)S(1)}, s32[2,13]{1,0:T(2,128)}, u32[]{:S(2)}) copy-start(s32[2,13]{1,0:T(2,128)} %param.15) | copy-start | bytes 316
  6.5 4.7 %copy-start.12 = (s32[2,13,4,256]{3,2,1,0:T(4,128)S(1)}, s32[2,13,4,256]{3,2,1,0:T(4,128)}, u32[]{:S(2)}) copy-start(s32[2,13,4,256]{3,2,1,0:T(4,128)} %param.13) | copy-start | bytes 319492
  6.5 5.6 %copy-start.9 = (bf16[2,13,4,256]{3,2,1,0:T(4,128)(2,1)S(1)}, bf16[2,13,4,256]{3,2,1,0:T(4,128)(2,1)}, u32[]{:S(2)}) copy-start(bf16[2,13,4,256]{3,2,1,0:T(4,128)(2,1)} %param.12) | copy-start | bytes 159748
  6.5 133.8 %all-reduce.2.cloned.1.call-start = ((), (), s32[]{:S(2)}) async-start(), calls=%async_computation | async-start | bytes 393216 | tf_op jit(solution)/shard_map/psum | solution.py:32
  8.6 131.7 %copy-start.5 = (bf16[48,1024]{1,0:T(8,128)(2,1)S(1)}, bf16[48,1024]{1,0:T(8,128)(2,1)}, u32[]{:S(2)}) copy-start(bf16[48,1024]{1,0:T(8,128)(2,1)} %param.9) | copy-start | bytes 294916
  142.9 1.6 copy-start.10
  144.4 6.6 %collective-permute-start = (bf16[48,2,256]{2,1,0:T(2,128)(2,1)}, bf16[48,2,256]{2,1,0:T(2,128)(2,1)}, u32[]{:S(2)}, u32[]{:S(2)}) collective-permute-start(bf16[48,2,256]{2,1,0:T(2,128)(2,1)} %reshape.74), channel_id=1, source_target_pairs={{0,1},{1,2},{2,3},{3,4},{4,5},{5,6},{6,7},{7,8},{8,9},{9,10},{10,1... | collective-permute-start | bytes 147464 | tf_op jit(solution)/shard_map/ppermute | solution.py:56
  144.5 7.5 %collective-permute-start.1 = (bf16[48,2,256]{2,1,0:T(2,128)(2,1)}, bf16[48,2,256]{2,1,0:T(2,128)(2,1)}, u32[]{:S(2)}, u32[]{:S(2)}) collective-permute-start(bf16[48,2,256]{2,1,0:T(2,128)(2,1)} %reshape.74), channel_id=1, source_target_pairs={{0,15},{1,0},{2,1},{3,2},{4,3},{5,4},{6,5},{7,6},{8,7},{9,8},{10,9... | collective-permute-start | bytes 147464 | tf_op jit(solution)/shard_map/ppermute | solution.py:61
  152.0 6.6 %collective-permute-start.2 = (bf16[48,2,256]{2,1,0:T(2,128)(2,1)}, bf16[48,2,256]{2,1,0:T(2,128)(2,1)}, u32[]{:S(2)}, u32[]{:S(2)}) collective-permute-start(bf16[48,2,256]{2,1,0:T(2,128)(2,1)} %collective-permute-done), channel_id=1, source_target_pairs={{0,1},{1,2},{2,3},{3,4},{4,5},{5,6},{6,7},{7,8},{8,9},{9,10},{10,1... | collective-permute-start | bytes 147464 | tf_op jit(solution)/shard_map/ppermute | solution.py:56
  153.0 6.6 %collective-permute-start.3 = (bf16[48,2,256]{2,1,0:T(2,128)(2,1)}, bf16[48,2,256]{2,1,0:T(2,128)(2,1)}, u32[]{:S(2)}, u32[]{:S(2)}) collective-permute-start(bf16[48,2,256]{2,1,0:T(2,128)(2,1)} %collective-permute-done.1), channel_id=1, source_target_pairs={{0,15},{1,0},{2,1},{3,2},{4,3},{5,4},{6,5},{7,6},{8,7},{9,8},{10,9... | collective-permute-start | bytes 147464 | tf_op jit(solution)/shard_map/ppermute | solution.py:61
  159.5 6.6 %collective-permute-start.4 = (bf16[48,2,256]{2,1,0:T(2,128)(2,1)}, bf16[48,2,256]{2,1,0:T(2,128)(2,1)}, u32[]{:S(2)}, u32[]{:S(2)}) collective-permute-start(bf16[48,2,256]{2,1,0:T(2,128)(2,1)} %collective-permute-done.2), channel_id=1, source_target_pairs={{0,1},{1,2},{2,3},{3,4},{4,5},{5,6},{6,7},{7,8},{8,9},{9,10},{10,1... | collective-permute-start | bytes 147464 | tf_op jit(solution)/shard_map/ppermute | solution.py:56
  160.6 6.6 %collective-permute-start.5 = (bf16[48,2,256]{2,1,0:T(2,128)(2,1)}, bf16[48,2,256]{2,1,0:T(2,128)(2,1)}, u32[]{:S(2)}, u32[]{:S(2)}) collective-permute-start(bf16[48,2,256]{2,1,0:T(2,128)(2,1)} %collective-permute-done.3), channel_id=1, source_target_pairs={{0,15},{1,0},{2,1},{3,2},{4,3},{5,4},{6,5},{7,6},{8,7},{9,8},{10,9... | collective-permute-start | bytes 147464 | tf_op jit(solution)/shard_map/ppermute | solution.py:61
  167.1 6.6 %collective-permute-start.6 = (bf16[48,2,256]{2,1,0:T(2,128)(2,1)}, bf16[48,2,256]{2,1,0:T(2,128)(2,1)}, u32[]{:S(2)}, u32[]{:S(2)}) collective-permute-start(bf16[48,2,256]{2,1,0:T(2,128)(2,1)} %collective-permute-done.4), channel_id=1, source_target_pairs={{0,1},{1,2},{2,3},{3,4},{4,5},{5,6},{6,7},{7,8},{8,9},{9,10},{10,1... | collective-permute-start | bytes 147464 | tf_op jit(solution)/shard_map/ppermute | solution.py:56
  168.1 6.6 %collective-permute-start.7 = (bf16[48,2,256]{2,1,0:T(2,128)(2,1)}, bf16[48,2,256]{2,1,0:T(2,128)(2,1)}, u32[]{:S(2)}, u32[]{:S(2)}) collective-permute-start(bf16[48,2,256]{2,1,0:T(2,128)(2,1)} %collective-permute-done.5), channel_id=1, source_target_pairs={{0,15},{1,0},{2,1},{3,2},{4,3},{5,4},{6,5},{7,6},{8,7},{9,8},{10,9... | collective-permute-start | bytes 147464 | tf_op jit(solution)/shard_map/ppermute | solution.py:61
  174.6 6.6 %collective-permute-start.8 = (bf16[48,2,256]{2,1,0:T(2,128)(2,1)}, bf16[48,2,256]{2,1,0:T(2,128)(2,1)}, u32[]{:S(2)}, u32[]{:S(2)}) collective-permute-start(bf16[48,2,256]{2,1,0:T(2,128)(2,1)} %collective-permute-done.6), channel_id=1, source_target_pairs={{0,1},{1,2},{2,3},{3,4},{4,5},{5,6},{6,7},{7,8},{8,9},{9,10},{10,1... | collective-permute-start | bytes 147464 | tf_op jit(solution)/shard_map/ppermute | solution.py:56
  175.6 6.6 %collective-permute-start.9 = (bf16[48,2,256]{2,1,0:T(2,128)(2,1)}, bf16[48,2,256]{2,1,0:T(2,128)(2,1)}, u32[]{:S(2)}, u32[]{:S(2)}) collective-permute-start(bf16[48,2,256]{2,1,0:T(2,128)(2,1)} %collective-permute-done.7), channel_id=1, source_target_pairs={{0,15},{1,0},{2,1},{3,2},{4,3},{5,4},{6,5},{7,6},{8,7},{9,8},{10,9... | collective-permute-start | bytes 147464 | tf_op jit(solution)/shard_map/ppermute | solution.py:61
  182.1 6.6 %collective-permute-start.10 = (bf16[48,2,256]{2,1,0:T(2,128)(2,1)}, bf16[48,2,256]{2,1,0:T(2,128)(2,1)}, u32[]{:S(2)}, u32[]{:S(2)}) collective-permute-start(bf16[48,2,256]{2,1,0:T(2,128)(2,1)} %collective-permute-done.8), channel_id=1, source_target_pairs={{0,1},{1,2},{2,3},{3,4},{4,5},{5,6},{6,7},{7,8},{8,9},{9,10},{10,1... | collective-permute-start | bytes 147464 | tf_op jit(solution)/shard_map/ppermute | solution.py:56
  183.2 6.6 %collective-permute-start.11 = (bf16[48,2,256]{2,1,0:T(2,128)(2,1)}, bf16[48,2,256]{2,1,0:T(2,128)(2,1)}, u32[]{:S(2)}, u32[]{:S(2)}) collective-permute-start(bf16[48,2,256]{2,1,0:T(2,128)(2,1)} %collective-permute-done.9), channel_id=1, source_target_pairs={{0,15},{1,0},{2,1},{3,2},{4,3},{5,4},{6,5},{7,6},{8,7},{9,8},{10,9... | collective-permute-start | bytes 147464 | tf_op jit(solution)/shard_map/ppermute | solution.py:61
  189.7 6.6 %collective-permute-start.12 = (bf16[48,2,256]{2,1,0:T(2,128)(2,1)}, bf16[48,2,256]{2,1,0:T(2,128)(2,1)}, u32[]{:S(2)}, u32[]{:S(2)}) collective-permute-start(bf16[48,2,256]{2,1,0:T(2,128)(2,1)} %collective-permute-done.10), channel_id=1, source_target_pairs={{0,1},{1,2},{2,3},{3,4},{4,5},{5,6},{6,7},{7,8},{8,9},{9,10},{10,1... | collective-permute-start | bytes 147464 | tf_op jit(solution)/shard_map/ppermute | solution.py:56
  190.7 6.6 %collective-permute-start.13 = (bf16[48,2,256]{2,1,0:T(2,128)(2,1)}, bf16[48,2,256]{2,1,0:T(2,128)(2,1)}, u32[]{:S(2)}, u32[]{:S(2)}) collective-permute-start(bf16[48,2,256]{2,1,0:T(2,128)(2,1)} %collective-permute-done.11), channel_id=1, source_target_pairs={{0,15},{1,0},{2,1},{3,2},{4,3},{5,4},{6,5},{7,6},{8,7},{9,8},{10,9... | collective-permute-start | bytes 147464 | tf_op jit(solution)/shard_map/ppermute | solution.py:61
  197.2 6.6 %collective-permute-start.14 = (bf16[48,2,256]{2,1,0:T(2,128)(2,1)}, bf16[48,2,256]{2,1,0:T(2,128)(2,1)}, u32[]{:S(2)}, u32[]{:S(2)}) collective-permute-start(bf16[48,2,256]{2,1,0:T(2,128)(2,1)} %collective-permute-done.12), channel_id=1, source_target_pairs={{0,1},{1,2},{2,3},{3,4},{4,5},{5,6},{6,7},{7,8},{8,9},{9,10},{10,1... | collective-permute-start | bytes 147464 | tf_op jit(solution)/shard_map/ppermute | solution.py:56
  247.2 14.2 %copy-start.7 = (f32[2,13,256]{2,1,0:T(8,128)S(1)}, f32[2,13,256]{2,1,0:T(8,128)}, u32[]{:S(2)}) copy-start(f32[2,13,256]{2,1,0:T(8,128)} %get-tuple-element.29) | copy-start | bytes 79876
  247.2 14.2 %copy-start.13 = (pred[2,13,256]{2,1,0:T(8,128)(4,1)S(1)}, pred[2,13,256]{2,1,0:T(8,128)(4,1)}, u32[]{:S(2)}) copy-start(pred[2,13,256]{2,1,0:T(8,128)(4,1)} %copy.226) | copy-start | bytes 19972
  247.2 19.7 %copy-start.8 = (f32[2,13,256]{2,1,0:T(8,128)S(1)}, f32[2,13,256]{2,1,0:T(8,128)}, u32[]{:S(2)}) copy-start(f32[2,13,256]{2,1,0:T(8,128)} %get-tuple-element.30) | copy-start | bytes 79876
  247.2 19.7 %copy-start.14 = (pred[2,13,256]{2,1,0:T(8,128)(4,1)S(1)}, pred[2,13,256]{2,1,0:T(8,128)(4,1)}, u32[]{:S(2)}) copy-start(pred[2,13,256]{2,1,0:T(8,128)(4,1)} %copy.220) | copy-start | bytes 19972
  261.4 11.0 %copy-start.4 = (bf16[6656,48]{1,0:T(8,128)(2,1)S(1)}, bf16[6656,48]{1,0:T(8,128)(2,1)}, u32[]{:S(2)}) copy-start(bf16[6656,48]{1,0:T(8,128)(2,1)} %gather_fusion) | copy-start | bytes 1916932
  261.4 11.0 %copy-start.6 = (f32[2,13,256]{2,1,0:T(8,128)S(1)}, f32[2,13,256]{2,1,0:T(8,128)}, u32[]{:S(2)}) copy-start(f32[2,13,256]{2,1,0:T(8,128)} %get-tuple-element.31) | copy-start | bytes 79876
  261.4 11.0 %copy-start.15 = (pred[2,13,256]{2,1,0:T(8,128)(4,1)S(1)}, pred[2,13,256]{2,1,0:T(8,128)(4,1)}, u32[]{:S(2)}) copy-start(pred[2,13,256]{2,1,0:T(8,128)(4,1)} %copy.196) | copy-start | bytes 19972
  266.9 8.0 %copy-start.3 = (bf16[6656,48]{1,0:T(8,128)(2,1)S(1)}, bf16[6656,48]{1,0:T(8,128)(2,1)}, u32[]{:S(2)}) copy-start(bf16[6656,48]{1,0:T(8,128)(2,1)} %gather_fusion.3) | copy-start | bytes 1916932
  266.9 8.0 %copy-start.16 = (pred[2,13,256]{2,1,0:T(8,128)(4,1)S(1)}, pred[2,13,256]{2,1,0:T(8,128)(4,1)}, u32[]{:S(2)}) copy-start(pred[2,13,256]{2,1,0:T(8,128)(4,1)} %copy.232) | copy-start | bytes 19972
  277.9 7.2 %collective-permute-start.15 = (bf16[48,2,256]{0,2,1:T(8,128)(2,1)S(1)}, bf16[48,2,256]{0,2,1:T(8,128)(2,1)S(1)}, u32[]{:S(2)}, u32[]{:S(2)}) collective-permute-start(bf16[48,2,256]{0,2,1:T(8,128)(2,1)S(1)} %get-tuple-element.7), channel_id=1, source_target_pairs={{0,1},{1,2},{2,3},{3,4},{4,5},{5,6},{6,7},{7,8},{8,9},{9,10},{10,1... | collective-permute-start | bytes 147464 | tf_op jit(solution)/shard_map/ppermute | solution.py:56
  277.9 7.2 %collective-permute-start.16 = (bf16[48,2,256]{0,2,1:T(8,128)(2,1)S(1)}, bf16[48,2,256]{0,2,1:T(8,128)(2,1)S(1)}, u32[]{:S(2)}, u32[]{:S(2)}) collective-permute-start(bf16[48,2,256]{0,2,1:T(8,128)(2,1)S(1)} %get-tuple-element.7), channel_id=1, source_target_pairs={{0,15},{1,0},{2,1},{3,2},{4,3},{5,4},{6,5},{7,6},{8,7},{9,8},{10,9... | collective-permute-start | bytes 147464 | tf_op jit(solution)/shard_map/ppermute | solution.py:61
  285.1 7.2 %collective-permute-start.17 = (bf16[48,2,256]{0,2,1:T(8,128)(2,1)S(1)}, bf16[48,2,256]{0,2,1:T(8,128)(2,1)S(1)}, u32[]{:S(2)}, u32[]{:S(2)}) collective-permute-start(bf16[48,2,256]{0,2,1:T(8,128)(2,1)S(1)} %collective-permute-done.15), channel_id=1, source_target_pairs={{0,1},{1,2},{2,3},{3,4},{4,5},{5,6},{6,7},{7,8},{8,9},{9,10},{10,1... | collective-permute-start | bytes 147464 | tf_op jit(solution)/shard_map/ppermute | solution.py:56
  285.1 7.2 %collective-permute-start.18 = (bf16[48,2,256]{0,2,1:T(8,128)(2,1)S(1)}, bf16[48,2,256]{0,2,1:T(8,128)(2,1)S(1)}, u32[]{:S(2)}, u32[]{:S(2)}) collective-permute-start(bf16[48,2,256]{0,2,1:T(8,128)(2,1)S(1)} %collective-permute-done.16), channel_id=1, source_target_pairs={{0,15},{1,0},{2,1},{3,2},{4,3},{5,4},{6,5},{7,6},{8,7},{9,8},{10,9... | collective-permute-start | bytes 147464 | tf_op jit(solution)/shard_map/ppermute | solution.py:61
  292.3 7.2 %collective-permute-start.19 = (bf16[48,2,256]{0,2,1:T(8,128)(2,1)S(1)}, bf16[48,2,256]{0,2,1:T(8,128)(2,1)S(1)}, u32[]{:S(2)}, u32[]{:S(2)}) collective-permute-start(bf16[48,2,256]{0,2,1:T(8,128)(2,1)S(1)} %collective-permute-done.17), channel_id=1, source_target_pairs={{0,1},{1,2},{2,3},{3,4},{4,5},{5,6},{6,7},{7,8},{8,9},{9,10},{10,1... | collective-permute-start | bytes 147464 | tf_op jit(solution)/shard_map/ppermute | solution.py:56
  292.3 7.2 %collective-permute-start.20 = (bf16[48,2,256]{0,2,1:T(8,128)(2,1)S(1)}, bf16[48,2,256]{0,2,1:T(8,128)(2,1)S(1)}, u32[]{:S(2)}, u32[]{:S(2)}) collective-permute-start(bf16[48,2,256]{0,2,1:T(8,128)(2,1)S(1)} %collective-permute-done.18), channel_id=1, source_target_pairs={{0,15},{1,0},{2,1},{3,2},{4,3},{5,4},{6,5},{7,6},{8,7},{9,8},{10,9... | collective-permute-start | bytes 147464 | tf_op jit(solution)/shard_map/ppermute | solution.py:61
  299.5 7.2 %collective-permute-start.21 = (bf16[48,2,256]{0,2,1:T(8,128)(2,1)S(1)}, bf16[48,2,256]{0,2,1:T(8,128)(2,1)S(1)}, u32[]{:S(2)}, u32[]{:S(2)}) collective-permute-start(bf16[48,2,256]{0,2,1:T(8,128)(2,1)S(1)} %collective-permute-done.19), channel_id=1, source_target_pairs={{0,1},{1,2},{2,3},{3,4},{4,5},{5,6},{6,7},{7,8},{8,9},{9,10},{10,1... | collective-permute-start | bytes 147464 | tf_op jit(solution)/shard_map/ppermute | solution.py:56
  299.5 7.2 %collective-permute-start.22 = (bf16[48,2,256]{0,2,1:T(8,128)(2,1)S(1)}, bf16[48,2,256]{0,2,1:T(8,128)(2,1)S(1)}, u32[]{:S(2)}, u32[]{:S(2)}) collective-permute-start(bf16[48,2,256]{0,2,1:T(8,128)(2,1)S(1)} %collective-permute-done.20), channel_id=1, source_target_pairs={{0,15},{1,0},{2,1},{3,2},{4,3},{5,4},{6,5},{7,6},{8,7},{9,8},{10,9... | collective-permute-start | bytes 147464 | tf_op jit(solution)/shard_map/ppermute | solution.py:61
  306.7 7.2 %collective-permute-start.23 = (bf16[48,2,256]{0,2,1:T(8,128)(2,1)S(1)}, bf16[48,2,256]{0,2,1:T(8,128)(2,1)S(1)}, u32[]{:S(2)}, u32[]{:S(2)}) collective-permute-start(bf16[48,2,256]{0,2,1:T(8,128)(2,1)S(1)} %collective-permute-done.21), channel_id=1, source_target_pairs={{0,1},{1,2},{2,3},{3,4},{4,5},{5,6},{6,7},{7,8},{8,9},{9,10},{10,1... | collective-permute-start | bytes 147464 | tf_op jit(solution)/shard_map/ppermute | solution.py:56
  306.7 7.2 %collective-permute-start.24 = (bf16[48,2,256]{0,2,1:T(8,128)(2,1)S(1)}, bf16[48,2,256]{0,2,1:T(8,128)(2,1)S(1)}, u32[]{:S(2)}, u32[]{:S(2)}) collective-permute-start(bf16[48,2,256]{0,2,1:T(8,128)(2,1)S(1)} %collective-permute-done.22), channel_id=1, source_target_pairs={{0,15},{1,0},{2,1},{3,2},{4,3},{5,4},{6,5},{7,6},{8,7},{9,8},{10,9... | collective-permute-start | bytes 147464 | tf_op jit(solution)/shard_map/ppermute | solution.py:61
  313.8 7.2 %collective-permute-start.25 = (bf16[48,2,256]{0,2,1:T(8,128)(2,1)S(1)}, bf16[48,2,256]{0,2,1:T(8,128)(2,1)S(1)}, u32[]{:S(2)}, u32[]{:S(2)}) collective-permute-start(bf16[48,2,256]{0,2,1:T(8,128)(2,1)S(1)} %collective-permute-done.23), channel_id=1, source_target_pairs={{0,1},{1,2},{2,3},{3,4},{4,5},{5,6},{6,7},{7,8},{8,9},{9,10},{10,1... | collective-permute-start | bytes 147464 | tf_op jit(solution)/shard_map/ppermute | solution.py:56
  313.9 7.2 %collective-permute-start.26 = (bf16[48,2,256]{0,2,1:T(8,128)(2,1)S(1)}, bf16[48,2,256]{0,2,1:T(8,128)(2,1)S(1)}, u32[]{:S(2)}, u32[]{:S(2)}) collective-permute-start(bf16[48,2,256]{0,2,1:T(8,128)(2,1)S(1)} %collective-permute-done.24), channel_id=1, source_target_pairs={{0,15},{1,0},{2,1},{3,2},{4,3},{5,4},{6,5},{7,6},{8,7},{9,8},{10,9... | collective-permute-start | bytes 147464 | tf_op jit(solution)/shard_map/ppermute | solution.py:61
  321.0 7.1 %collective-permute-start.27 = (bf16[48,2,256]{0,2,1:T(8,128)(2,1)S(1)}, bf16[48,2,256]{0,2,1:T(8,128)(2,1)S(1)}, u32[]{:S(2)}, u32[]{:S(2)}) collective-permute-start(bf16[48,2,256]{0,2,1:T(8,128)(2,1)S(1)} %collective-permute-done.25), channel_id=1, source_target_pairs={{0,1},{1,2},{2,3},{3,4},{4,5},{5,6},{6,7},{7,8},{8,9},{9,10},{10,1... | collective-permute-start | bytes 147464 | tf_op jit(solution)/shard_map/ppermute | solution.py:56
  321.1 7.1 %collective-permute-start.28 = (bf16[48,2,256]{0,2,1:T(8,128)(2,1)S(1)}, bf16[48,2,256]{0,2,1:T(8,128)(2,1)S(1)}, u32[]{:S(2)}, u32[]{:S(2)}) collective-permute-start(bf16[48,2,256]{0,2,1:T(8,128)(2,1)S(1)} %collective-permute-done.26), channel_id=1, source_target_pairs={{0,15},{1,0},{2,1},{3,2},{4,3},{5,4},{6,5},{7,6},{8,7},{9,8},{10,9... | collective-permute-start | bytes 147464 | tf_op jit(solution)/shard_map/ppermute | solution.py:61
  328.1 7.1 %collective-permute-start.29 = (bf16[48,2,256]{0,2,1:T(8,128)(2,1)S(1)}, bf16[48,2,256]{0,2,1:T(8,128)(2,1)S(1)}, u32[]{:S(2)}, u32[]{:S(2)}) collective-permute-start(bf16[48,2,256]{0,2,1:T(8,128)(2,1)S(1)} %collective-permute-done.27), channel_id=1, source_target_pairs={{0,1},{1,2},{2,3},{3,4},{4,5},{5,6},{6,7},{7,8},{8,9},{9,10},{10,1... | collective-permute-start | bytes 147464 | tf_op jit(solution)/shard_map/ppermute | solution.py:56
  391.8 11.0 %copy-start.2 = (bf16[6656,48]{1,0:T(8,128)(2,1)S(1)}, bf16[6656,48]{1,0:T(8,128)(2,1)}, u32[]{:S(2)}) copy-start(bf16[6656,48]{1,0:T(8,128)(2,1)} %gather_fusion.4) | copy-start | bytes 1916932
  397.3 7.9 %copy-start.1 = (bf16[6656,48]{1,0:T(8,128)(2,1)S(1)}, bf16[6656,48]{1,0:T(8,128)(2,1)}, u32[]{:S(2)}) copy-start(bf16[6656,48]{1,0:T(8,128)(2,1)} %gather_fusion.7) | copy-start | bytes 1916932
  405.2 2.6 copy-start.11
Sparse Core Ops, SparseCore 0:
  12.9 127.3 all-reduce.1
